TPU v7x, 256 devices: a whole 4x4x8 slice. The times are simulated.
256 devices in a mesh: field: 2 (over z_hi), dom: 128 (over z_lo, y, x, core).
Axes of the slice: x: 4, y: 4, z: 8 (z_hi: 2, z_lo: 4; z = z_hi * 4 + z_lo), core: 2. Of those that a mesh axis runs over, the one named last changes fastest.
Arguments:
- state: float32 [9, 35, 32768], P(None, None, ('field', 'dom')), may hold values from -6 to 6
- star: float32 [3, 9, 9, 32768], P(None, None, None, ('field', 'dom')), may hold values from -2.4 to 2.4
- normals: float32 [4, 3, 32768], P(None, None, ('field', 'dom')), may hold values from -3.6 to 3.6
- speed: float32 [32768], P(('field', 'dom')), may hold values from 0.5 to 2
- stiffness: float32 [3, 35, 35], replicated, may hold values from -1 to 1
- face_proj: float32 [4, 35, 15], replicated, may hold values from -1 to 1
- face_lift: float32 [4, 15, 35], replicated, may hold values from -0.75 to 0.75
- rotations: float32 [3, 15, 15], replicated, may hold values from -1.5 to 1.5
- face_source: int32 [4, 32768], P(None, ('field', 'dom')), may hold values from 0 to 624, as said below
- face_orient: int32 [4, 32768], P(None, ('field', 'dom')), may hold values from 0 to 2
- halo_send: int32 [2, 8192], P(None, ('field', 'dom')), may hold values from 0 to 511
- partner_send: int32 [3, 4096], P(None, ('field', 'dom')), may hold values from 0 to 511
Outputs:
- state_out: float32 [9, 35, 32768], P(None, None, ('field', 'dom'))
Inputs may be any that keep to these rules, and one draw needn't show every extreme that they name: `face_source`: positions 512 to 623 of a device's list are each read by exactly one face of that device, and every device has a face that reads the zero trace at 624.
All inputs are finite; a program needn't handle non-finite values.
Results may differ from a plain program's by a relative error of at most 0.0003.
Values sent between devices are 32-bit elements; how exact they have to be, the bound alone decides.
A program may use at most 64 MiB of HBM per device.

v0:
```python
import functools

import jax
import jax.numpy as jnp
from jax import lax
from jax.experimental import pallas as pl
from jax.experimental.pallas import tpu as pltpu
from jax.sharding import PartitionSpec as P

Q, B, FB, NE = 9, 35, 15, 128
BP, LP = 40, 48
F32, BF16 = jnp.float32, jnp.bfloat16
HALF = 0.5
ROUTES = (
    (0, 32, 32, -1, False),
    (32, 32, 0, 1, False),
    (64, 16, 96, -1, True),
    (80, 16, 80, 0, True),
    (96, 16, 64, 1, True),
)


def coefs(t0, t1):
    out, fact = [], 1.0
    for k in range(5):
        fact *= k + 1
        out.append((t1 ** (k + 1) - t0 ** (k + 1)) / fact)
    return out


EARLY, LATE = coefs(0.0, HALF), coefs(HALF, 2 * HALF)


def split(x):
    hi = x.astype(BF16)
    return hi, (x - hi.astype(F32)).astype(BF16)


def mm(a, b):
    return jnp.dot(a, b, preferred_element_type=F32)


def kernel(
    state, star, normals, speed, stiff, proj, lift, rot, fsrc, forient, halo, part,
    out,
    d_buf, cur, integ, a_pred, a_vol, a_proj, a_lift, a_rot, pad, ipad,
    sel_send, sel_loc, sel_rem, fmat, trace, both_g, gath, flux, vol, send, recv,
    send_sem, recv_sem,
):
    g, i = lax.axis_index("field"), lax.axis_index("dom")
    count = lax.axis_size("dom")
    before, after = lax.rem(i + count - 1, count), lax.rem(i + 1, count)

    def device(step, other):
        return ((1 - g) if other else g, {-1: before, 0: i, 1: after}[step])

    barrier = pltpu.get_barrier_semaphore()
    for _, _, _, step, other in ROUTES:
        pl.semaphore_signal(barrier, inc=1, device_id=device(step, other),
                            device_id_type=pl.DeviceIdType.MESH)

    zrow = jnp.zeros((BP - B, NE), F32)
    for q in range(Q):
        s = jnp.concatenate([state[q], zrow], axis=0)
        d_buf[0, q] = s
        cur[q] = s
        integ[q, BP:LP] = jnp.zeros((LP - BP, NE), F32)

    pad[...] = jnp.zeros_like(pad)
    for d in range(3):
        pad[d, 0:B, 0:B] = stiff[d]
    pred = jnp.zeros((BP, 128), F32)
    volm = jnp.zeros((BP, 128), F32)
    for d in range(3):
        x = pad[d]
        xt = x.T[0:BP]
        x = x[0:BP]
        pred = pred - (pltpu.roll(xt, BP * d, 1) if d else xt)
        volm = volm + (pltpu.roll(x, BP * d, 1) if d else x)

    def put_wide(dst, m):
        hi, lo = split(m)
        z = jnp.zeros_like(lo)
        dst[...] = jnp.concatenate(
            [jnp.concatenate([hi, hi], axis=1), jnp.concatenate([lo, z], axis=1)], axis=0)

    def put_narrow(dst, m, width):
        hi, lo = split(m)
        hi2 = (hi.astype(F32) + pltpu.roll(hi.astype(F32), width, 1)).astype(BF16)
        dst[...] = jnp.concatenate([hi2, lo], axis=0)

    put_wide(a_pred, pred)
    put_wide(a_vol, volm)
    for f in range(4):
        pad[f] = jnp.zeros((128, 128), F32)
        pad[f, 0:B, 0:FB] = proj[f]
    rows = [pad[f].T[0:16] for f in range(4)]
    put_narrow(a_proj, jnp.concatenate(rows, axis=0), LP)
    m = jnp.zeros((BP, 128), F32)
    for f in range(4):
        pad[f] = jnp.zeros((128, 128), F32)
        pad[f, 0:FB, 0:B] = lift[f]
        x = pad[f].T[0:BP]
        m = m + (pltpu.roll(x, 16 * f, 1) if f else x)
    put_narrow(a_lift, m, 64)
    m = jnp.zeros((16, 128), F32)
    for h in range(3):
        pad[h] = jnp.zeros((128, 128), F32)
        pad[h, 0:FB, 0:FB] = rot[h]
        x = pad[h].T[0:16]
        m = m + (pltpu.roll(x, 16 * h, 1) if h else x)
    put_narrow(a_rot, m, 48)

    ipad[...] = jnp.full((8, 128), -1, jnp.int32)
    ipad[0:2, 0:32] = halo[...]
    ipad[2:5, 0:16] = part[...]
    rows8 = ipad[...]
    want = rows8[0:1]
    for r, off in ((1, 32), (2, 64), (3, 80), (4, 96)):
        want = jnp.maximum(want, pltpu.roll(rows8, off, 1)[r:r + 1])
    iota = lax.broadcasted_iota(jnp.int32, (512, 128), 0)
    sel_send[...] = jnp.where(iota == want, 1.0, 0.0).astype(BF16)
    riota = iota[0:128]
    not_first = jnp.where(i > 0, 1, 0)
    not_last = jnp.where(i < count - 1, 1, 0)
    low = (riota < 32) | ((riota >= 64) & (riota < 80))
    high = ((riota >= 32) & (riota < 64)) | ((riota >= 96) & (riota < 112))
    mid = (riota >= 80) & (riota < 96)
    live = jnp.where(low, not_first, jnp.where(high, not_last, jnp.where(mid, 1, 0)))
    rpos = jnp.where(live > 0, riota + 512, -1)
    for f in range(4):
        src = fsrc[f:f + 1, :]
        sel_loc[:, f * 128:(f + 1) * 128] = jnp.where(iota == src, 1.0, 0.0).astype(BF16)
        sel_rem[:, f * 128:(f + 1) * 128] = jnp.where(rpos == src, 1.0, 0.0).astype(BF16)

    for f in range(4):
        n = [0.5 * normals[f, d:d + 1, :] for d in range(3)]
        for q in range(Q):
            fmat[q, 0:Q, f * 128:(f + 1) * 128] = (
                n[0] * star[0, q] + n[1] * star[1, q] + n[2] * star[2, q])

    def star_apply(value, mat, emit):
        v = [value(p) for p in range(Q)]
        zpad = jnp.zeros((8, NE), F32)
        for q0 in range(0, Q, 2):
            qs = [q for q in (q0, q0 + 1) if q < Q]
            cols = []
            for q in qs:
                parts = []
                for d in range(3):
                    acc = star[d, q, 0:1, :] * v[0]
                    for p in range(1, Q):
                        acc = acc + star[d, q, p:p + 1, :] * v[p]
                    parts.append(acc)
                hi, lo = split(jnp.concatenate(parts + [zpad], axis=0))
                cols.append(jnp.concatenate([hi, lo], axis=0))
            x = cols[0] if len(cols) == 1 else jnp.concatenate(cols, axis=1)
            r = mm(mat, x)
            r = r[0:BP] + r[BP:2 * BP]
            for n, q in enumerate(qs):
                emit(q, r[:, n * NE:(n + 1) * NE])

    def copies(s):
        out_ = []
        for k, (r0, n, d0, step, other) in enumerate(ROUTES):
            out_.append(pltpu.make_async_remote_copy(
                src_ref=send.at[s, pl.ds(r0, n)],
                dst_ref=recv.at[s, pl.ds(d0, n)],
                send_sem=send_sem.at[s, k],
                recv_sem=recv_sem.at[s, k],
                device_id=device(step, other),
                device_id_type=pl.DeviceIdType.MESH,
            ))
        return out_

    for s in range(2):
        ocean = g == 0

        def coef(k):
            if s == 0:
                return EARLY[k]
            return jnp.where(ocean, LATE[k], EARLY[k]).astype(F32)

        if s == 1:
            for q in range(Q):
                st = jnp.concatenate([state[q], zrow], axis=0)
                d_buf[0, q] = jnp.where(ocean, st, cur[q])
        c0 = coef(0)
        for q in range(Q):
            integ[q, 0:BP] = c0 * d_buf[0, q]

        def level(k, _):
            here, there = lax.rem(k, 2), lax.rem(k + 1, 2)
            c = jnp.float32(0.0)
            for n in range(4):
                c = jnp.where(k == n, coef(n + 1), c)

            def emit(q, r):
                d_buf[there, q] = r
                integ[q, 0:BP] = integ[q, 0:BP] + c * r

            star_apply(lambda p: d_buf[here, p], a_pred[...], emit)
            return 0

        lax.fori_loop(0, 4, level, 0)

        for q0 in range(0, Q, 2):
            qs = [q for q in (q0, q0 + 1) if q < Q]
            cols = []
            for q in qs:
                hi, lo = split(integ[q])
                cols.append(jnp.concatenate([hi, lo, jnp.zeros((32, NE), BF16)], axis=0))
            x = cols[0] if len(cols) == 1 else jnp.concatenate(cols, axis=1)
            r = mm(a_proj[...], x)
            r = r[0:64] + r[64:128]
            for n, q in enumerate(qs):
                for f in range(4):
                    t = r[f * 16:(f + 1) * 16, n * NE:(n + 1) * NE]
                    trace[q, :, f * 128:(f + 1) * 128] = t
                    hi, lo = split(t)
                    both_g[q * 16:(q + 1) * 16, f * 128:(f + 1) * 128] = hi
                    both_g[144 + q * 16:144 + (q + 1) * 16, f * 128:(f + 1) * 128] = lo
        r = mm(both_g[...], sel_send[...])
        r = jnp.concatenate([r[0:144] + r[144:288], jnp.zeros((112, 128), F32)], axis=0)
        send[s] = r.T
        if s == 0:
            pl.semaphore_wait(barrier, len(ROUTES))
        ops = copies(s)
        for op in ops:
            op.start()

        gath[...] = mm(both_g[...], sel_loc[...])

        def emit_vol(q, r):
            cur[q] = cur[q] + r

        star_apply(lambda p: integ[p, 0:BP], a_vol[...], emit_vol)

        for op in ops:
            op.wait_recv()
        rt = jnp.concatenate([recv[s], jnp.zeros((16, 256), F32)], axis=0).T[0:144]
        hi, lo = split(rt)
        gath[...] = gath[...] + mm(jnp.concatenate([hi, lo], axis=0), sel_rem[...])

        for q in range(Q):
            ghi = gath[q * 16:(q + 1) * 16]
            glo = gath[144 + q * 16:144 + (q + 1) * 16]
            masked = []
            for x in (ghi, glo):
                for h in range(3):
                    hit = jnp.concatenate([forient[f:f + 1, :] for f in range(4)], axis=1) == h
                    masked.append(jnp.where(hit, x, 0.0).astype(BF16))
            masked.append(jnp.zeros((32, 512), BF16))
            r = mm(a_rot[...], jnp.concatenate(masked, axis=0))
            nb = r[0:16] + r[16:32]
            gath[q * 16:(q + 1) * 16] = trace[q] + nb
            gath[144 + q * 16:144 + (q + 1) * 16] = trace[q] - nb
        sp = 0.5 * speed[...].reshape(1, NE)
        for f in range(4):
            ln = slice(f * 128, (f + 1) * 128)
            sums = [gath[p * 16:(p + 1) * 16, ln] for p in range(Q)]
            for q in range(Q):
                acc = sp * gath[144 + q * 16:144 + (q + 1) * 16, ln]
                for p in range(Q):
                    acc = acc + fmat[q, p:p + 1, ln] * sums[p]
                hi, lo = split(acc)
                flux[f * 16:(f + 1) * 16, q * NE:(q + 1) * NE] = hi
                flux[64 + f * 16:64 + (f + 1) * 16, q * NE:(q + 1) * NE] = lo
        r = mm(a_lift[...], flux[...])
        r = r[0:BP] + r[BP:2 * BP]
        for q in range(Q):
            new = cur[q] - r[:, q * NE:(q + 1) * NE]
            if s == 0:
                cur[q] = new
            else:
                out[q] = new[0:B]
    for s in range(2):
        for op in copies(s):
            op.wait_send()


def local(*args):
    vmem = pl.BlockSpec(memory_space=pltpu.VMEM)
    scratch = [
        pltpu.VMEM((2, Q, BP, NE), F32),
        pltpu.VMEM((Q, BP, NE), F32),
        pltpu.VMEM((Q, LP, NE), F32),
        pltpu.VMEM((2 * BP, 256), BF16),
        pltpu.VMEM((2 * BP, 256), BF16),
        pltpu.VMEM((128, 128), BF16),
        pltpu.VMEM((2 * BP, 128), BF16),
        pltpu.VMEM((32, 128), BF16),
        pltpu.VMEM((4, 128, 128), F32),
        pltpu.VMEM((8, 128), jnp.int32),
        pltpu.VMEM((512, 128), BF16),
        pltpu.VMEM((512, 512), BF16),
        pltpu.VMEM((128, 512), BF16),
        pltpu.VMEM((Q, 16, 512), F32),
        pltpu.VMEM((Q, 16, 512), F32),
        pltpu.VMEM((288, 512), BF16),
        pltpu.VMEM((288, 512), F32),
        pltpu.VMEM((128, Q * NE), BF16),
        pltpu.VMEM((8, 128), F32),
        pltpu.VMEM((2, 128, 256), F32),
        pltpu.VMEM((2, 112, 256), F32),
        pltpu.SemaphoreType.DMA((2, 5)),
        pltpu.SemaphoreType.DMA((2, 5)),
    ]
    return pl.pallas_call(
        kernel,
        out_shape=jax.ShapeDtypeStruct((Q, B, NE), F32),
        in_specs=[vmem] * len(args),
        out_specs=vmem,
        scratch_shapes=scratch,
        compiler_params=pltpu.CompilerParams(
            collective_id=0, has_side_effects=True, vmem_limit_bytes=32 * 1024 * 1024),
    )(*args)


def solution(mesh):
    in_specs = (
        P(None, None, ("field", "dom")),
        P(None, None, None, ("field", "dom")),
        P(None, None, ("field", "dom")),
        P(("field", "dom")),
        P(),
        P(),
        P(),
        P(),
        P(None, ("field", "dom")),
        P(None, ("field", "dom")),
        P(None, ("field", "dom")),
        P(None, ("field", "dom")),
    )
    out_specs = P(None, None, ("field", "dom"))
    return jax.shard_map(local, mesh=mesh, in_specs=in_specs, out_specs=out_specs, check_vma=False)
```

profile of v0, /device:TPU:64, one launch (start us, length us, event | category | flops | bytes accessed | tf_op | source)
XLA Modules:
  0.0 31.7 jit_solution(8385890528074000045)
XLA Ops:
  0.0 0.0 copy-start.8
  0.0 0.7 %copy.14.normals = f32[4,3,128]{2,1,0:T(4,128)S(1)} copy(f32[4,3,128]{2,0,1:T(4,128)} %param.14) | data formatting | bytes 12288 | tf_op args[2]
  0.7 0.8 %copy.16.lift = f32[4,15,35]{2,1,0:T(8,128)S(1)} copy(f32[4,15,35]{2,0,1:T(4,128)} %param.18) | data formatting | bytes 16800 | tf_op args[6]
  1.5 0.9 %copy.15.proj = f32[4,35,15]{2,1,0:T(8,128)S(1)} copy(f32[4,35,15]{1,0,2:T(4,128)} %param.17) | data formatting | bytes 16800 | tf_op args[5]
  2.4 0.0 copy-done.8
  2.4 0.0 copy-start
  2.4 0.0 copy-start.1
  2.4 0.0 copy-start.2
  2.4 0.0 copy-start.3
  2.4 0.0 copy-start.4
  2.4 0.0 copy-start.5
  2.4 0.0 copy-start.6
  2.4 0.0 copy-start.7
  2.5 0.8 %copy-done = f32[9,35,128]{2,1,0:T(8,128)S(1)} copy-done((f32[9,35,128]{2,1,0:T(8,128)S(1)}, f32[9,35,128]{2,1,0:T(8,128)}, u32[]{:S(2)}) %copy-start) | copy-done | bytes 161304
  3.3 0.0 copy-done.1
  3.3 0.0 copy-done.2
  3.3 0.0 copy-done.3
  3.3 0.0 copy-done.4
  3.3 0.0 copy-done.5
  3.3 0.0 copy-done.6
  3.3 0.0 copy-done.7
  3.3 27.7 %shard_map.118 = f32[9,35,128]{2,1,0:T(8,128)S(1)} custom-call(f32[9,35,128]{2,1,0:T(8,128)S(1)} %copy-done, f32[3,9,9,128]{3,2,1,0:T(8,128)S(1)} %copy.13.star, f32[4,3,128]{2,1,0:T(4,128)S(1)} %copy.14.normals, f32[128]{0:T(128)S(1)} %copy-done.7, f32[3,35,35]{2,1,0:T(8,128)S(1)} %copy-done.1, f32[4,35,15]{2,1,0:T(8,128)S(1)} %copy.15.proj, ...), custom_call_target="tpu_custom_call" | custom-call | tf_op jit(solution)/shard_map/pallas_call | solution.py:309
  31.0 0.7 %copy.18 = f32[9,35,128]{2,1,0:T(8,128)} copy(f32[9,35,128]{2,1,0:T(8,128)S(1)} %shard_map.118) | data formatting | bytes 322560
  (1 shorter events, 0.0 us)
Async XLA Ops:
  0.0 2.4 %copy-start.8 = (f32[3,9,9,128]{3,0,2,1:T(4,128)S(1)}, f32[3,9,9,128]{3,0,2,1:T(4,128)}, u32[]{:S(2)}) copy-start(f32[3,9,9,128]{3,0,2,1:T(4,128)} %param.13) | copy-start | bytes 373252
  2.4 0.9 %copy-start = (f32[9,35,128]{2,1,0:T(8,128)S(1)}, f32[9,35,128]{2,1,0:T(8,128)}, u32[]{:S(2)}) copy-start(f32[9,35,128]{2,1,0:T(8,128)} %state.1) | copy-start | bytes 483844
  2.4 0.9 %copy-start.1 = (f32[3,35,35]{2,1,0:T(8,128)S(1)}, f32[3,35,35]{2,1,0:T(8,128)}, u32[]{:S(2)}) copy-start(f32[3,35,35]{2,1,0:T(8,128)} %stiff.1) | copy-start | bytes 44104
  2.4 0.9 %copy-start.2 = (f32[3,15,15]{2,1,0:T(8,128)S(1)}, f32[3,15,15]{2,1,0:T(8,128)}, u32[]{:S(2)}) copy-start(f32[3,15,15]{2,1,0:T(8,128)} %rot.1) | copy-start | bytes 8104
  2.4 0.9 %copy-start.3 = (s32[4,128]{1,0:T(4,128)S(1)}, s32[4,128]{1,0:T(4,128)}, u32[]{:S(2)}) copy-start(s32[4,128]{1,0:T(4,128)} %fsrc.1) | copy-start | bytes 6148
  2.4 0.9 %copy-start.4 = (s32[4,128]{1,0:T(4,128)S(1)}, s32[4,128]{1,0:T(4,128)}, u32[]{:S(2)}) copy-start(s32[4,128]{1,0:T(4,128)} %forient.1) | copy-start | bytes 6148
  2.4 0.9 %copy-start.5 = (s32[3,16]{1,0:T(4,128)S(1)}, s32[3,16]{1,0:T(4,128)}, u32[]{:S(2)}) copy-start(s32[3,16]{1,0:T(4,128)} %part.1) | copy-start | bytes 580
  2.4 0.9 %copy-start.6 = (s32[2,32]{1,0:T(2,128)S(1)}, s32[2,32]{1,0:T(2,128)}, u32[]{:S(2)}) copy-start(s32[2,32]{1,0:T(2,128)} %halo.1) | copy-start | bytes 772
  2.4 0.9 %copy-start.7 = (f32[128]{0:T(128)S(1)}, f32[128]{0:T(128)}, u32[]{:S(2)}) copy-start(f32[128]{0:T(128)} %speed.1) | copy-start | bytes 1540
where the time goes:
time: 31.9 us; the launch traced here: 31.7 us
  Pallas kernels  27.7 us (87%)
  local copies, waits for them, and re-layouts  3.9 us (12%)
    pallas_call x1, Pallas kernels, local(): pl.pallas_call(kernel, out_shape=jax.ShapeDtypeStruct((Q, B, NE), F32), i...  27.7 us
    unnamed x23, local copies, waits for them, and re-layouts  3.9 us

commit v1 on v0

--- a/solution.py
+++ b/solution.py
@@ -92,14 +92,14 @@
     put_wide(a_pred, pred)
     put_wide(a_vol, volm)
     for f in range(4):
-        pad[f] = jnp.zeros((128, 128), F32)
-        pad[f, 0:B, 0:FB] = proj[f]
-    rows = [pad[f].T[0:16] for f in range(4)]
+        pad[f, 0:16] = jnp.zeros((16, 128), F32)
+        pad[f, 0:FB, 0:B] = proj[:, f, :]
+    rows = [pad[f, 0:16] for f in range(4)]
     put_narrow(a_proj, jnp.concatenate(rows, axis=0), LP)
     m = jnp.zeros((BP, 128), F32)
     for f in range(4):
         pad[f] = jnp.zeros((128, 128), F32)
-        pad[f, 0:FB, 0:B] = lift[f]
+        pad[f, 0:FB, 0:B] = lift[:, f, :]
         x = pad[f].T[0:BP]
         m = m + (pltpu.roll(x, 16 * f, 1) if f else x)
     put_narrow(a_lift, m, 64)
@@ -134,10 +134,10 @@
         sel_rem[:, f * 128:(f + 1) * 128] = jnp.where(rpos == src, 1.0, 0.0).astype(BF16)
 
     for f in range(4):
-        n = [0.5 * normals[f, d:d + 1, :] for d in range(3)]
+        n = [0.5 * normals[d, f:f + 1, :] for d in range(3)]
         for q in range(Q):
             fmat[q, 0:Q, f * 128:(f + 1) * 128] = (
-                n[0] * star[0, q] + n[1] * star[1, q] + n[2] * star[2, q])
+                n[0] * star[q, :, 0, :] + n[1] * star[q, :, 1, :] + n[2] * star[q, :, 2, :])
 
     def star_apply(value, mat, emit):
         v = [value(p) for p in range(Q)]
@@ -148,9 +148,9 @@
             for q in qs:
                 parts = []
                 for d in range(3):
-                    acc = star[d, q, 0:1, :] * v[0]
+                    acc = star[q, 0, d:d + 1, :] * v[0]
                     for p in range(1, Q):
-                        acc = acc + star[d, q, p:p + 1, :] * v[p]
+                        acc = acc + star[q, p, d:d + 1, :] * v[p]
                     parts.append(acc)
                 hi, lo = split(jnp.concatenate(parts + [zpad], axis=0))
                 cols.append(jnp.concatenate([hi, lo], axis=0))
@@ -279,7 +279,10 @@
             op.wait_send()
 
 
-def local(*args):
+def local(state, star, normals, speed, stiff, proj, lift, rot, fsrc, forient, halo, part):
+    args = (
+        state, star.transpose(1, 2, 0, 3), normals.transpose(1, 0, 2), speed, stiff,
+        proj.transpose(2, 0, 1), lift.transpose(1, 0, 2), rot, fsrc, forient, halo, part)
     vmem = pl.BlockSpec(memory_space=pltpu.VMEM)
     scratch = [
         pltpu.VMEM((2, Q, BP, NE), F32),

time: 31.9 us -> 36.5 us (1.14)
  local copies, waits for them, and re-layouts: 3.9 us -> 8.32 us
    unnamed x23 -> x25, local copies, waits for them, and re-layouts: 3.9 us -> 8.32 us
where the time goes in v1:
time: 36.5 us; the launch traced here: 36 us
  Pallas kernels  27.7 us (76%)
  local copies, waits for them, and re-layouts  8.32 us (23%)
    pallas_call x1, Pallas kernels, local(): pl.pallas_call(kernel, out_shape=jax.ShapeDtypeStruct((Q, B, NE), F32), i...  27.7 us
    unnamed x25, local copies, waits for them, and re-layouts  8.32 us

profile of v1, /device:TPU:64, one launch (start us, length us, event | category | flops | bytes accessed | tf_op | source)
XLA Modules:
  0.0 36.0 jit_solution(10146587128260532854)
XLA Ops:
  0.0 0.0 copy-start.6
  0.0 0.0 copy-start.10
  0.0 0.0 copy-start.11
  0.0 0.7 %copy-done.6 = f32[4,3,128]{2,0,1:T(4,128)S(1)} copy-done((f32[4,3,128]{2,0,1:T(4,128)S(1)}, f32[4,3,128]{2,0,1:T(4,128)}, u32[]{:S(2)}) %copy-start.6) | copy-done | bytes 6168
  0.7 0.0 copy-done.10
  0.7 0.0 copy-done.11
  0.7 0.0 copy-start
  0.7 0.9 %copy-done = f32[9,35,128]{2,1,0:T(8,128)S(1)} copy-done((f32[9,35,128]{2,1,0:T(8,128)S(1)}, f32[9,35,128]{2,1,0:T(8,128)}, u32[]{:S(2)}) %copy-start) | copy-done | bytes 161304
  1.6 0.0 copy-start.1
  1.6 0.9 %copy-done.1 = f32[3,9,9,128]{3,0,2,1:T(4,128)S(1)} copy-done((f32[3,9,9,128]{3,0,2,1:T(4,128)S(1)}, f32[3,9,9,128]{3,0,2,1:T(4,128)}, u32[]{:S(2)}) %copy-start.1) | copy-done | bytes 124440
  2.5 0.0 copy-start.2
  2.5 0.8 %copy-done.2 = f32[3,35,35]{2,1,0:T(8,128)S(1)} copy-done((f32[3,35,35]{2,1,0:T(8,128)S(1)}, f32[3,35,35]{2,1,0:T(8,128)}, u32[]{:S(2)}) %copy-start.2) | copy-done | bytes 14724
  3.4 0.0 copy-start.3
  3.4 0.8 %copy-done.3 = f32[4,35,15]{1,0,2:T(4,128)S(1)} copy-done((f32[4,35,15]{1,0,2:T(4,128)S(1)}, f32[4,35,15]{1,0,2:T(4,128)}, u32[]{:S(2)}) %copy-start.3) | copy-done | bytes 8424
  4.1 0.0 copy-start.4
  4.1 0.8 %copy-done.4 = f32[4,15,35]{2,0,1:T(4,128)S(1)} copy-done((f32[4,15,35]{2,0,1:T(4,128)S(1)}, f32[4,15,35]{2,0,1:T(4,128)}, u32[]{:S(2)}) %copy-start.4) | copy-done | bytes 8424
  4.9 0.0 copy-start.5
  4.9 0.7 %copy-done.5 = f32[3,15,15]{2,1,0:T(8,128)S(1)} copy-done((f32[3,15,15]{2,1,0:T(8,128)S(1)}, f32[3,15,15]{2,1,0:T(8,128)}, u32[]{:S(2)}) %copy-start.5) | copy-done | bytes 2724
  5.6 0.0 copy-start.7
  5.6 0.7 %copy-done.7 = s32[4,128]{1,0:T(4,128)S(1)} copy-done((s32[4,128]{1,0:T(4,128)S(1)}, s32[4,128]{1,0:T(4,128)}, u32[]{:S(2)}) %copy-start.7) | copy-done | bytes 2072
  6.3 0.0 copy-start.8
  6.3 0.7 %copy-done.8 = s32[4,128]{1,0:T(4,128)S(1)} copy-done((s32[4,128]{1,0:T(4,128)S(1)}, s32[4,128]{1,0:T(4,128)}, u32[]{:S(2)}) %copy-start.8) | copy-done | bytes 2072
  7.0 0.0 copy-start.9
  7.0 0.7 %copy-done.9 = s32[3,16]{1,0:T(4,128)S(1)} copy-done((s32[3,16]{1,0:T(4,128)S(1)}, s32[3,16]{1,0:T(4,128)}, u32[]{:S(2)}) %copy-start.9) | copy-done | bytes 216
  7.7 27.7 %shard_map.118 = f32[9,35,128]{2,1,0:T(8,128)S(1)} custom-call(f32[9,35,128]{2,1,0:T(8,128)S(1)} %copy-done, f32[9,9,3,128]{3,2,1,0:T(4,128)S(1)} %bitcast.4, f32[3,4,128]{2,1,0:T(4,128)S(1)} %bitcast.7, f32[128]{0:T(128)S(1)} %copy-done.11, f32[3,35,35]{2,1,0:T(8,128)S(1)} %copy-done.2, f32[15,4,35]{2,1,0:T(4,128)S(1)} %bitcast.5, ...), custom_call_target="tpu_custom_call" | custom-call | tf_op jit(solution)/shard_map/pallas_call | solution.py:312
  35.4 0.7 %copy.14 = f32[9,35,128]{2,1,0:T(8,128)} copy(f32[9,35,128]{2,1,0:T(8,128)S(1)} %shard_map.118) | data formatting | bytes 322560
Async XLA Ops:
  0.0 0.7 %copy-start.6 = (f32[4,3,128]{2,0,1:T(4,128)S(1)}, f32[4,3,128]{2,0,1:T(4,128)}, u32[]{:S(2)}) copy-start(f32[4,3,128]{2,0,1:T(4,128)} %param.14) | copy-start | bytes 18436
  0.0 0.7 %copy-start.10 = (s32[2,32]{1,0:T(2,128)S(1)}, s32[2,32]{1,0:T(2,128)}, u32[]{:S(2)}) copy-start(s32[2,32]{1,0:T(2,128)} %halo.1) | copy-start | bytes 772
  0.0 0.7 %copy-start.11 = (f32[128]{0:T(128)S(1)}, f32[128]{0:T(128)}, u32[]{:S(2)}) copy-start(f32[128]{0:T(128)} %speed.1) | copy-start | bytes 1540
  0.7 0.9 %copy-start = (f32[9,35,128]{2,1,0:T(8,128)S(1)}, f32[9,35,128]{2,1,0:T(8,128)}, u32[]{:S(2)}) copy-start(f32[9,35,128]{2,1,0:T(8,128)} %state.1) | copy-start | bytes 483844
  1.6 0.9 %copy-start.1 = (f32[3,9,9,128]{3,0,2,1:T(4,128)S(1)}, f32[3,9,9,128]{3,0,2,1:T(4,128)}, u32[]{:S(2)}) copy-start(f32[3,9,9,128]{3,0,2,1:T(4,128)} %param.13) | copy-start | bytes 373252
  2.5 0.8 %copy-start.2 = (f32[3,35,35]{2,1,0:T(8,128)S(1)}, f32[3,35,35]{2,1,0:T(8,128)}, u32[]{:S(2)}) copy-start(f32[3,35,35]{2,1,0:T(8,128)} %stiff.1) | copy-start | bytes 44104
  3.4 0.8 %copy-start.3 = (f32[4,35,15]{1,0,2:T(4,128)S(1)}, f32[4,35,15]{1,0,2:T(4,128)}, u32[]{:S(2)}) copy-start(f32[4,35,15]{1,0,2:T(4,128)} %param.17) | copy-start | bytes 25204
  4.1 0.8 %copy-start.4 = (f32[4,15,35]{2,0,1:T(4,128)S(1)}, f32[4,15,35]{2,0,1:T(4,128)}, u32[]{:S(2)}) copy-start(f32[4,15,35]{2,0,1:T(4,128)} %param.18) | copy-start | bytes 25204
  4.9 0.7 %copy-start.5 = (f32[3,15,15]{2,1,0:T(8,128)S(1)}, f32[3,15,15]{2,1,0:T(8,128)}, u32[]{:S(2)}) copy-start(f32[3,15,15]{2,1,0:T(8,128)} %rot.1) | copy-start | bytes 8104
  5.6 0.7 %copy-start.7 = (s32[4,128]{1,0:T(4,128)S(1)}, s32[4,128]{1,0:T(4,128)}, u32[]{:S(2)}) copy-start(s32[4,128]{1,0:T(4,128)} %fsrc.1) | copy-start | bytes 6148
  6.3 0.7 %copy-start.8 = (s32[4,128]{1,0:T(4,128)S(1)}, s32[4,128]{1,0:T(4,128)}, u32[]{:S(2)}) copy-start(s32[4,128]{1,0:T(4,128)} %forient.1) | copy-start | bytes 6148
  7.0 0.7 %copy-start.9 = (s32[3,16]{1,0:T(4,128)S(1)}, s32[3,16]{1,0:T(4,128)}, u32[]{:S(2)}) copy-start(s32[3,16]{1,0:T(4,128)} %part.1) | copy-start | bytes 580
